TPU v7x, 256 devices: a whole 4x4x8 slice. The times are simulated.
256 devices in a mesh: row: 16 (over x, y), col: 16 (over z, core).
Axes of the slice: x: 4, y: 4, z: 8, core: 2. Of those that a mesh axis runs over, the one named last changes fastest.
Arguments:
- target: float32 [8, 16, 128, 8, 16, 128], P(None, 'row', None, None, 'col'), may hold values from -6 to 6
- panel_a: bfloat16 [2, 32, 128, 512], P(None, 'col'), may hold values from -1.1953125 to 1.1953125
- inv_factor: bfloat16 [2, 512, 512], replicated, as said below
- panel_rhs: bfloat16 [2, 512, 256], P(None, 'col'), may hold values from -6 to 6
- panel_rows: int32 [2, 32], replicated, may hold values from 0 to 127, as said below
- right_sides: float32 [8, 16, 128, 256], P(None, 'col'), may hold values from -12 to 12
Outputs:
- updated_target: float32 [8, 16, 128, 8, 16, 128], P(None, 'row', None, None, 'col')
- updated_sides: float32 [8, 16, 128, 256], P(None, 'col')
Inputs may be any that keep to these rules, and one draw needn't show every extreme that they name: `panel_rows`: each row holds 32 distinct positions in increasing order, the first 0 and the last 127. `inv_factor`: lower triangular, diagonal between 0.5 and 2.
All inputs are finite; a program needn't handle non-finite values.
Results may differ from a plain program's by a relative error of at most 0.0035.
Values may be sent and summed in bfloat16 or wider, within the bound.
A program may use at most 128 MiB of HBM per device.

v0:
```python
import jax
import jax.numpy as jnp
from jax import lax
from jax.sharding import PartitionSpec as P


def shards(target, panel_a, inv_factor, panel_rhs, panel_rows, right_sides):
    row_count = lax.axis_size("row")
    col_count = lax.axis_size("col")
    row_index = lax.axis_index("row")
    col_index = lax.axis_index("col")
    tile_rows = target.shape[2]
    row_blocks = target.shape[0]
    col_blocks = target.shape[3]
    slab_rows = tile_rows // row_count
    shard_rows = panel_rhs.shape[1]
    updated_target = target
    updated_sides = right_sides
    row_places = jnp.arange(row_blocks, dtype=jnp.int32) * row_count + row_index
    col_places = jnp.arange(col_blocks, dtype=jnp.int32) * col_count + col_index
    for which_panel in range(2):
        factor = inv_factor[which_panel]
        positions = panel_rows[which_panel]
        own_rows = lax.dynamic_slice_in_dim(
            panel_a[which_panel], row_index * slab_rows, slab_rows, 1
        )
        solved_piece = jnp.einsum(
            "axq,pq->axp", own_rows, factor, preferred_element_type=jnp.float32
        ).astype(jnp.bfloat16)
        column_tiles = lax.all_gather(solved_piece, "row", axis=1, tiled=True)
        all_tiles = lax.all_gather(column_tiles, "col", axis=0, tiled=True)
        columns = lax.dynamic_slice_in_dim(factor, col_index * shard_rows, shard_rows, 1)
        local_term = jnp.dot(columns, panel_rhs[which_panel], preferred_element_type=jnp.float32)
        partial_value = lax.psum(local_term, "col").astype(jnp.bfloat16)
        pick_rows = (positions[None, :] == row_places[:, None]).astype(jnp.bfloat16)
        pick_cols = (positions[None, :] == col_places[:, None]).astype(jnp.bfloat16)
        row_set = jnp.einsum(
            "ia,axp->ixp", pick_rows, all_tiles, preferred_element_type=jnp.float32
        ).astype(jnp.bfloat16)
        col_set = jnp.einsum(
            "ka,axp->kxp", pick_cols, all_tiles, preferred_element_type=jnp.float32
        ).astype(jnp.bfloat16)
        schur_term = jnp.einsum(
            "ixp,kyp->ixky", row_set, col_set, preferred_element_type=jnp.float32
        )
        updated_target = updated_target - schur_term[:, None, :, :, None, :]
        side_term = jnp.einsum(
            "kxp,pn->kxn", col_set, partial_value, preferred_element_type=jnp.float32
        )
        updated_sides = updated_sides - side_term[:, None]
    return (updated_target, updated_sides)


def solution(mesh):
    placed = (
        P(None, "row", None, None, "col", None),
        P(None, "col", None, None),
        P(),
        P(None, "col", None),
        P(),
        P(None, "col", None, None),
    )
    return jax.shard_map(
        shards,
        mesh=mesh,
        in_specs=placed,
        out_specs=(P(None, "row", None, None, "col", None), P(None, "col", None, None)),
        check_vma=False,
    )
```

profile of v0, /device:TPU:0, one launch (start us, length us, event | category | flops | bytes accessed | tf_op | source)
XLA Modules:
  0.0 168.0 jit_solution(11555292527745360764)
XLA Ops:
  7.2 0.0 copy-start.4
  7.2 0.0 copy-start.5
  7.2 0.0 all-gather.5.cloned.1.call-start
  7.2 1.1 fusion.73
  8.3 1.3 convolution_convert_fusion
  9.6 24.2 %all_gather.14 = bf16[2,128,512]{2,1,0:T(8,128)(2,1)} all-gather(bf16[2,8,512]{2,1,0:T(8,128)(2,1)S(1)} %convolution_convert_fusion), channel_id=1, replica_groups=mesh['row'=16,'col'=16] {'row'}, dimensions={1}, use_global_device_ids=true | all-gather | bytes 278528 | tf_op jit(solution)/shard_map/all_gather | solution.py:30
  33.8 0.0 all-gather.5.cloned.1.call-update
  33.8 0.0 all-gather.3.cloned.1.call-start
  33.9 1.3 convolution_convert_fusion.1
  35.2 25.0 %all_gather.12 = bf16[2,128,512]{2,1,0:T(8,128)(2,1)} all-gather(bf16[2,8,512]{2,1,0:T(8,128)(2,1)S(1)} %convolution_convert_fusion.1), channel_id=1, replica_groups=mesh['row'=16,'col'=16] {'row'}, dimensions={1}, use_global_device_ids=true | all-gather | bytes 278528 | tf_op jit(solution)/shard_map/all_gather | solution.py:30
  60.2 0.0 all-gather.3.cloned.1.call-update
  60.2 1.3 fusion.72
  61.5 0.0 copy-done.4
  61.5 0.3 fusion.34
  61.8 0.3 fusion.36
  62.1 0.0 copy-done.5
  62.1 69.4 %all-reduce.2 = (bf16[512,256]{1,0:T(8,128)(2,1)S(1)}, bf16[512,256]{1,0:T(8,128)(2,1)S(1)}) all-reduce(f32[512,256]{1,0:T(8,128)S(1)} %fusion.34, f32[512,256]{1,0:T(8,128)S(1)} %fusion.36), channel_id=1, replica_groups=mesh['row'=16,'col'=16] {'col'}, use_global_device_ids=true, to_apply=%region_1.0 | all-reduce | flops 262144 | bytes 1572864 | tf_op jit(solution)/shard_map/psum | solution.py:34
  131.6 0.0 all-gather.5.cloned.1.call-done
  131.6 4.5 %fusion.11 = bf16[8,128,512]{2,0,1:T(8,128)(2,1)S(1)} fusion(bf16[32,128,512]{2,1,0:T(8,128)(2,1)} %all-gather.5.cloned.1.call-done, s32[32]{0:T(128)S(1)} %get-tuple-element.12, s32[8]{0:T(128)S(1)} %fusion.68), kind=kOutput, calls=%fused_computation.13 | convolution fusion | flops 34078976 | bytes 5243040 | tf_op jit(solution)/shard_map/ka,axp->kxp/dot_general | solution.py:40
  136.2 1.7 %convolution_bitcast_fusion = f32[8,1,128,256]{3,2,0,1:T(8,128)} fusion(bf16[8,128,512]{2,0,1:T(8,128)(2,1)S(1)} %fusion.11, bf16[512,256]{1,0:T(8,128)(2,1)S(1)} %get-tuple-element.6), kind=kOutput, calls=%fused_computation.14 | convolution fusion | flops 268435456 | bytes 2359296 | tf_op jit(solution)/shard_map/kxp,pn->kxn/dot_general | solution.py:47
  137.9 0.0 all-gather.3.cloned.1.call-done
  137.9 0.0 copy-start.1
  137.9 4.7 %fusion.8 = bf16[8,128,512]{2,0,1:T(8,128)(2,1)S(1)} fusion(bf16[32,128,512]{2,1,0:T(8,128)(2,1)} %all-gather.3.cloned.1.call-done, s32[32]{0:T(128)S(1)} %get-tuple-element.13, s32[8]{0:T(128)S(1)} %fusion.68), kind=kOutput, calls=%fused_computation.12 | convolution fusion | flops 34078976 | bytes 5243040 | tf_op jit(solution)/shard_map/ka,axp->kxp/dot_general | solution.py:40
  142.6 0.0 copy-done.1
  142.6 2.4 %fusion.4 = bf16[8,128,512]{2,0,1:T(8,128)(2,1)S(1)} fusion(bf16[32,128,512]{2,1,0:T(8,128)(2,1)S(1)} %copy-done.1, s32[32]{0:T(128)S(1)} %get-tuple-element.13, s32[8]{0:T(128)S(1)} %fusion.69), kind=kOutput, calls=%fused_computation.6 | convolution fusion | flops 33554688 | bytes 5243040 | tf_op jit(solution)/shard_map/ia,axp->ixp/dot_general | solution.py:37
  145.0 0.0 copy-start
  145.0 1.6 fusion.18
  146.6 0.5 copy-done
  147.2 0.0 copy-start.2
  147.2 2.4 %fusion = bf16[8,128,512]{2,0,1:T(8,128)(2,1)S(1)} fusion(bf16[32,128,512]{2,1,0:T(8,128)(2,1)S(1)} %copy-done, s32[32]{0:T(128)S(1)} %get-tuple-element.12, s32[8]{0:T(128)S(1)} %fusion.69), kind=kOutput, calls=%fused_computation.2 | convolution fusion | flops 33554688 | bytes 5243040 | tf_op jit(solution)/shard_map/ia,axp->ixp/dot_general | solution.py:37
  149.5 0.0 copy-done.2
  149.5 2.4 %bitcast_subtract_fusion = f32[8,1,128,8,1,128]{5,2,3,0,4,1:T(8,128)S(1)} fusion(f32[8,128,8,128]{3,1,2,0:T(8,128)S(1)} %fusion.18, f32[8,1,128,8,1,128]{5,4,3,2,1,0:T(1,128)S(1)} %copy-done.2, bf16[8,128,512]{2,0,1:T(8,128)(2,1)S(1)} %fusion, bf16[8,128,512]{2,0,1:T(8,128)(2,1)S(1)} %fusion.11), kind=kOutput, calls=%fused_computation | convolution fusion | flops 1075838976 | bytes 14680064 | tf_op jit(solution)/shard_map/ixp,kyp->ixky/dot_general | solution.py:43
  151.9 0.0 copy-start.3
  151.9 6.3 %copy.26 = f32[8,1,128,8,1,128]{5,4,3,2,1,0:T(1,128)} copy(f32[8,1,128,8,1,128]{5,2,3,0,4,1:T(8,128)S(1)} %bitcast_subtract_fusion) | data formatting | bytes 8388608
  158.2 0.0 copy-done.3
  158.2 2.9 %fusion.16 = f32[8,1,128,256]{3,2,1,0:T(8,128)} fusion(f32[8,1,128,256]{3,2,0,1:T(8,128)S(1)} %copy-done.3, f32[8,1,128,256]{3,2,1,0:T(8,128)} %param.11, bf16[8,128,512]{2,0,1:T(8,128)(2,1)S(1)} %fusion.8, bf16[512,256]{1,0:T(8,128)(2,1)S(1)} %get-tuple-element.7), kind=kOutput, calls=%fused_computation.18 | convolution fusion | flops 268959744 | bytes 4456448 | tf_op jit(solution)/shard_map/kxp,pn->kxn/dot_general | solution.py:47
  (3 shorter events, 0.0 us)
Async XLA Ops:
  7.2 54.3 %copy-start.4 = (bf16[2,32,256]{2,1,0:T(8,128)(2,1)S(1)}, bf16[2,32,256]{2,1,0:T(8,128)(2,1)}, u32[]{:S(2)}) copy-start(bf16[2,32,256]{2,1,0:T(8,128)(2,1)} %param.9) | copy-start | bytes 98308
  7.2 54.9 %copy-start.5 = (s32[2,32]{1,0:T(2,128)S(1)}, s32[2,32]{1,0:T(2,128)}, u32[]{:S(2)}) copy-start(s32[2,32]{1,0:T(2,128)} %param.10) | copy-start | bytes 772
  7.2 124.4 %all-gather.5.cloned.1.call-start = ((), (), s32[]{:S(2)}) async-start(), calls=%async_computation.1 | async-start | bytes 4456448 | tf_op jit(solution)/shard_map/all_gather | solution.py:31
  33.8 104.1 %all-gather.3.cloned.1.call-start = ((), (), s32[]{:S(2)}) async-start(), calls=%async_computation | async-start | bytes 4456448 | tf_op jit(solution)/shard_map/all_gather | solution.py:31
  137.9 4.7 %copy-start.1 = (bf16[32,128,512]{2,1,0:T(8,128)(2,1)S(1)}, bf16[32,128,512]{2,1,0:T(8,128)(2,1)}, u32[]{:S(2)}) copy-start(bf16[32,128,512]{2,1,0:T(8,128)(2,1)} %all-gather.3.cloned.1.call-done) | copy-start | bytes 12582916
  145.0 2.2 %copy-start = (bf16[32,128,512]{2,1,0:T(8,128)(2,1)S(1)}, bf16[32,128,512]{2,1,0:T(8,128)(2,1)}, u32[]{:S(2)}) copy-start(bf16[32,128,512]{2,1,0:T(8,128)(2,1)} %all-gather.5.cloned.1.call-done) | copy-start | bytes 12582916
  147.2 2.4 %copy-start.2 = (f32[8,1,128,8,1,128]{5,4,3,2,1,0:T(1,128)S(1)}, f32[8,1,128,8,1,128]{5,4,3,2,1,0:T(1,128)}, u32[]{:S(2)}) copy-start(f32[8,1,128,8,1,128]{5,4,3,2,1,0:T(1,128)} %param.6) | copy-start | bytes 12582916
  151.9 6.3 %copy-start.3 = (f32[8,1,128,256]{3,2,0,1:T(8,128)S(1)}, f32[8,1,128,256]{3,2,0,1:T(8,128)}, u32[]{:S(2)}) copy-start(f32[8,1,128,256]{3,2,0,1:T(8,128)} %convolution_bitcast_fusion) | copy-start | bytes 3145732
Sparse Core Ops, SparseCore 0:
  33.9 43.4 all-gather.4
  79.3 43.1 all-gather.2
where the time goes:
time: 168 us
  blocking collectives  119 us (71%)
  matrix products  25.8 us (15%)
  between operations  14.2 us (8%)
  local copies, waits for them, and re-layouts  9.27 us (6%)
    psum x1, blocking collectives, shards(): partial_value = lax.psum(local_term, 'col').astype(jnp.bfloat16)  69.4 us
    all_gather x2, blocking collectives, shards(): column_tiles = lax.all_gather(solved_piece, 'row', axis=1, tiled=True)  49.2 us
    dot_general x2, matrix products, shards(): jnp.einsum('ka,axp->kxp', pick_cols, all_tiles, preferred_element_type=jn...  9.25 us
    unnamed x13, local copies, waits for them, and re-layouts  6.89 us
    dot_general x2, matrix products, shards(): jnp.einsum('ia,axp->ixp', pick_rows, all_tiles, preferred_element_type=jn...  4.72 us
    dot_general x2, matrix products, shards(): jnp.einsum('kxp,pn->kxn', col_set, partial_value, preferred_element_type=...  4.65 us
    dot_general x2, matrix products, shards(): jnp.einsum('ixp,kyp->ixky', row_set, col_set, preferred_element_type=jnp....  4 us
  transfers between devices with their start and end apart: 2, of which 0 were waited for; matrix products, arithmetic and copies ran while one was open for 6% of the time, Pallas kernels for 0%

commit v1 on v0

--- a/solution.py
+++ b/solution.py
@@ -27,7 +27,9 @@
         solved_piece = jnp.einsum(
             "axq,pq->axp", own_rows, factor, preferred_element_type=jnp.float32
         ).astype(jnp.bfloat16)
-        column_tiles = lax.all_gather(solved_piece, "row", axis=1, tiled=True)
+        column_tiles = jnp.concatenate(
+            lax.all_to_all(jnp.stack([solved_piece] * lax.axis_size("row")), "row", 0, 0), axis=1
+        )
         all_tiles = lax.all_gather(column_tiles, "col", axis=0, tiled=True)
         columns = lax.dynamic_slice_in_dim(factor, col_index * shard_rows, shard_rows, 1)
         local_term = jnp.dot(columns, panel_rhs[which_panel], preferred_element_type=jnp.float32)

time: 168 us -> 149 us (0.89)
  blocking collectives: 119 us -> 98.9 us
    all_gather x2 -> x0, blocking collectives: 49.2 us -> none  [shards(): column_tiles = lax.all_gather(solved_piece, 'row', axis=1, tiled=True)]
    all_to_all x0 -> x2, blocking collectives: none -> 25.5 us  [shards(): lax.all_to_all(jnp.stack([solved_piece] * lax.axis_size('row')), 'row', 0...]
    psum x1, blocking collectives: 69.4 us -> 73.4 us  [shards(): partial_value = lax.psum(local_term, 'col').astype(jnp.bfloat16)]
    unnamed x13 -> x15, local copies, waits for them, and re-layouts: 6.89 us -> 6.89 us
where the time goes in v1:
time: 149 us
  blocking collectives  98.9 us (66%)
  matrix products  25.7 us (17%)
  between operations  14.2 us (10%)
  local copies, waits for them, and re-layouts  9.61 us (6%)
    psum x1, blocking collectives, shards(): partial_value = lax.psum(local_term, 'col').astype(jnp.bfloat16)  73.4 us
    all_to_all x2, blocking collectives, shards(): lax.all_to_all(jnp.stack([solved_piece] * lax.axis_size('row')), 'row', 0...  25.5 us
    dot_general x2, matrix products, shards(): jnp.einsum('ka,axp->kxp', pick_cols, all_tiles, preferred_element_type=jn...  9.25 us
    unnamed x15, local copies, waits for them, and re-layouts  6.89 us
    dot_general x2, matrix products, shards(): jnp.einsum('ia,axp->ixp', pick_rows, all_tiles, preferred_element_type=jn...  4.72 us
    dot_general x2, matrix products, shards(): jnp.einsum('kxp,pn->kxn', col_set, partial_value, preferred_element_type=...  4.64 us
    dot_general x2, matrix products, shards(): jnp.einsum('ixp,kyp->ixky', row_set, col_set, preferred_element_type=jnp....  3.96 us
  transfers between devices with their start and end apart: 2, of which 0 were waited for; matrix products, arithmetic and copies ran while one was open for 6% of the time, Pallas kernels for 0%

profile of v1, /device:TPU:0, one launch (start us, length us, event | category | flops | bytes accessed | tf_op | source)
XLA Modules:
  0.0 148.6 jit_solution(8437274021383018492)
XLA Ops:
  7.2 0.0 copy-start.3
  7.2 0.0 copy-start.5
  7.2 0.0 all-gather.5.cloned.1.call-start
  7.2 0.0 copy-start.6
  7.2 1.1 fusion.83
  8.4 1.3 convolution_convert_fusion
  9.7 13.6 %all_to_all.10 = bf16[16,2,8,512]{3,2,1,0:T(8,128)(2,1)S(1)} all-to-all(bf16[16,2,8,512]{3,2,1,0:T(8,128)(2,1)S(1)} %stack.5), channel_id=1, replica_groups=mesh['row'=16,'col'=16] {'row'}, dimensions={0} | all-to-all | bytes 524288 | tf_op jit(solution)/shard_map/all_to_all | solution.py:31
  23.3 0.7 copy.103
  24.1 0.0 all-gather.5.cloned.1.call-update
  24.1 0.0 all-gather.3.cloned.1.call-start
  24.1 1.3 convolution_convert_fusion.1
  25.5 11.9 %all_to_all.11 = bf16[16,2,8,512]{3,2,1,0:T(8,128)(2,1)S(1)} all-to-all(bf16[16,2,8,512]{3,2,1,0:T(8,128)(2,1)S(1)} %stack.4), channel_id=1, replica_groups=mesh['row'=16,'col'=16] {'row'}, dimensions={0} | all-to-all | bytes 524288 | tf_op jit(solution)/shard_map/all_to_all | solution.py:31
  37.4 0.7 copy.104
  38.1 0.0 all-gather.3.cloned.1.call-update
  38.1 0.0 copy-done.3
  38.1 0.1 fusion.82
  38.2 0.0 copy-done.5
  38.2 0.3 fusion.44
  38.5 0.3 fusion.46
  38.8 0.0 copy-done.6
  38.8 73.4 %all-reduce.2 = (bf16[512,256]{1,0:T(8,128)(2,1)S(1)}, bf16[512,256]{1,0:T(8,128)(2,1)S(1)}) all-reduce(f32[512,256]{1,0:T(8,128)S(1)} %fusion.44, f32[512,256]{1,0:T(8,128)S(1)} %fusion.46), channel_id=1, replica_groups=mesh['row'=16,'col'=16] {'col'}, use_global_device_ids=true, to_apply=%region_1.0 | all-reduce | flops 262144 | bytes 1572864 | tf_op jit(solution)/shard_map/psum | solution.py:36
  112.2 0.0 all-gather.5.cloned.1.call-done
  112.3 4.5 %fusion.17 = bf16[8,128,512]{2,0,1:T(8,128)(2,1)S(1)} fusion(bf16[32,128,512]{2,1,0:T(8,128)(2,1)} %all-gather.5.cloned.1.call-done, s32[32]{0:T(128)S(1)} %get-tuple-element.16, s32[8]{0:T(128)S(1)} %fusion.78), kind=kOutput, calls=%fused_computation.13 | convolution fusion | flops 34078976 | bytes 5243040 | tf_op jit(solution)/shard_map/ka,axp->kxp/dot_general | solution.py:42
  116.8 1.7 %convolution_bitcast_fusion = f32[8,1,128,256]{3,2,0,1:T(8,128)} fusion(bf16[8,128,512]{2,0,1:T(8,128)(2,1)S(1)} %fusion.17, bf16[512,256]{1,0:T(8,128)(2,1)S(1)} %get-tuple-element.10), kind=kOutput, calls=%fused_computation.16 | convolution fusion | flops 268435456 | bytes 2359296 | tf_op jit(solution)/shard_map/kxp,pn->kxn/dot_general | solution.py:49
  118.5 0.0 all-gather.3.cloned.1.call-done
  118.5 0.0 copy-start.1
  118.5 4.7 %fusion.11 = bf16[8,128,512]{2,0,1:T(8,128)(2,1)S(1)} fusion(bf16[32,128,512]{2,1,0:T(8,128)(2,1)} %all-gather.3.cloned.1.call-done, s32[32]{0:T(128)S(1)} %get-tuple-element.17, s32[8]{0:T(128)S(1)} %fusion.78), kind=kOutput, calls=%fused_computation.11 | convolution fusion | flops 34078976 | bytes 5243040 | tf_op jit(solution)/shard_map/ka,axp->kxp/dot_general | solution.py:42
  123.2 0.0 copy-done.1
  123.2 2.4 %fusion.23 = bf16[8,128,512,1]{2,0,1,3:T(8,128)(2,1)S(1)} fusion(bf16[32,128,512]{2,1,0:T(8,128)(2,1)S(1)} %copy-done.1, s32[32]{0:T(128)S(1)} %get-tuple-element.17, s32[8]{0:T(128)S(1)} %fusion.79), kind=kOutput, calls=%fused_computation.15 | convolution fusion | flops 34078976 | bytes 5243040 | tf_op jit(solution)/shard_map/ia,axp->ixp/dot_general | solution.py:39
  125.6 0.0 copy-start
  125.6 1.6 %fusion.31 = f32[8,128,8,128]{3,1,2,0:T(8,128)S(1)} fusion(bf16[8,128,512,1]{2,0,1,3:T(8,128)(2,1)S(1)} %fusion.23, bf16[8,128,512]{2,0,1:T(8,128)(2,1)S(1)} %fusion.11), kind=kOutput, calls=%fused_computation.25 | convolution fusion | flops 1073741824 | bytes 6291456 | tf_op jit(solution)/shard_map/ixp,kyp->ixky/dot_general | solution.py:45
  127.3 0.5 copy-done
  127.8 0.0 copy-start.2
  127.8 2.4 %fusion.20 = bf16[8,128,512,1]{2,0,1,3:T(8,128)(2,1)S(1)} fusion(bf16[32,128,512]{2,1,0:T(8,128)(2,1)S(1)} %copy-done, s32[32]{0:T(128)S(1)} %get-tuple-element.16, s32[8]{0:T(128)S(1)} %fusion.79), kind=kOutput, calls=%fused_computation.14 | convolution fusion | flops 34078976 | bytes 5243040 | tf_op jit(solution)/shard_map/ia,axp->ixp/dot_general | solution.py:39
  130.2 0.0 copy-done.2
  130.2 2.3 %bitcast_subtract_fusion = f32[8,1,128,8,1,128]{5,2,3,0,4,1:T(8,128)S(1)} fusion(f32[8,128,8,128]{3,1,2,0:T(8,128)S(1)} %fusion.31, f32[8,1,128,8,1,128]{5,4,3,2,1,0:T(1,128)S(1)} %copy-done.2, bf16[8,128,512,1]{2,0,1,3:T(8,128)(2,1)S(1)} %fusion.20, bf16[8,128,512]{2,0,1:T(8,128)(2,1)S(1)} %fusion.17), kind=kOutput, calls=%fused_computation | convolution fusion | flops 1075838976 | bytes 14680064 | tf_op jit(solution)/shard_map/ixp,kyp->ixky/dot_general | solution.py:45
  132.5 0.0 copy-start.4
  132.5 6.3 %copy.56 = f32[8,1,128,8,1,128]{5,4,3,2,1,0:T(1,128)} copy(f32[8,1,128,8,1,128]{5,2,3,0,4,1:T(8,128)S(1)} %bitcast_subtract_fusion) | data formatting | bytes 8388608
  138.8 0.0 copy-done.4
  138.8 2.9 %fusion.28 = f32[8,1,128,256]{3,2,1,0:T(8,128)} fusion(f32[8,1,128,256]{3,2,0,1:T(8,128)S(1)} %copy-done.4, f32[8,1,128,256]{3,2,1,0:T(8,128)} %param.11, bf16[8,128,512]{2,0,1:T(8,128)(2,1)S(1)} %fusion.11, bf16[512,256]{1,0:T(8,128)(2,1)S(1)} %get-tuple-element.11), kind=kOutput, calls=%fused_computation.20 | convolution fusion | flops 268959744 | bytes 4456448 | tf_op jit(solution)/shard_map/kxp,pn->kxn/dot_general | solution.py:49
  (5 shorter events, 0.1 us)
Async XLA Ops:
  7.2 30.9 %copy-start.3 = (bf16[2,512,512]{2,1,0:T(8,128)(2,1)S(1)}, bf16[2,512,512]{2,1,0:T(8,128)(2,1)}, u32[]{:S(2)}) copy-start(bf16[2,512,512]{2,1,0:T(8,128)(2,1)} %param.8) | copy-start | bytes 3145732
  7.2 31.0 %copy-start.5 = (bf16[2,32,256]{2,1,0:T(8,128)(2,1)S(1)}, bf16[2,32,256]{2,1,0:T(8,128)(2,1)}, u32[]{:S(2)}) copy-start(bf16[2,32,256]{2,1,0:T(8,128)(2,1)} %param.9) | copy-start | bytes 98308
  7.2 105.1 %all-gather.5.cloned.1.call-start = ((), (), s32[]{:S(2)}) async-start(), calls=%async_computation.3 | async-start | bytes 4456448 | tf_op jit(solution)/shard_map/all_gather | solution.py:33
  7.2 31.6 %copy-start.6 = (s32[2,32]{1,0:T(2,128)S(1)}, s32[2,32]{1,0:T(2,128)}, u32[]{:S(2)}) copy-start(s32[2,32]{1,0:T(2,128)} %param.10) | copy-start | bytes 772
  24.1 94.4 %all-gather.3.cloned.1.call-start = ((), (), s32[]{:S(2)}) async-start(), calls=%async_computation.2 | async-start | bytes 4456448 | tf_op jit(solution)/shard_map/all_gather | solution.py:33
  118.5 4.7 %copy-start.1 = (bf16[32,128,512]{2,1,0:T(8,128)(2,1)S(1)}, bf16[32,128,512]{2,1,0:T(8,128)(2,1)}, u32[]{:S(2)}) copy-start(bf16[32,128,512]{2,1,0:T(8,128)(2,1)} %all-gather.3.cloned.1.call-done) | copy-start | bytes 12582916
  125.6 2.2 %copy-start = (bf16[32,128,512]{2,1,0:T(8,128)(2,1)S(1)}, bf16[32,128,512]{2,1,0:T(8,128)(2,1)}, u32[]{:S(2)}) copy-start(bf16[32,128,512]{2,1,0:T(8,128)(2,1)} %all-gather.5.cloned.1.call-done) | copy-start | bytes 12582916
  127.8 2.4 %copy-start.2 = (f32[8,1,128,8,1,128]{5,4,3,2,1,0:T(1,128)S(1)}, f32[8,1,128,8,1,128]{5,4,3,2,1,0:T(1,128)}, u32[]{:S(2)}) copy-start(f32[8,1,128,8,1,128]{5,4,3,2,1,0:T(1,128)} %param.6) | copy-start | bytes 12582916
  132.5 6.3 %copy-start.4 = (f32[8,1,128,256]{3,2,0,1:T(8,128)S(1)}, f32[8,1,128,256]{3,2,0,1:T(8,128)}, u32[]{:S(2)}) copy-start(f32[8,1,128,256]{3,2,0,1:T(8,128)} %convolution_bitcast_fusion) | copy-start | bytes 3145732
Sparse Core Ops, SparseCore 0:
  24.2 42.7 all-gather.4
  69.4 42.9 all-gather.2
